TPU v7x, 32 devices: a whole 2x2x4 slice. The times are simulated.
32 devices in a mesh: groups: 2 (over y), fsdp: 8 (over z, core), band: 2 (over x).
Axes of the slice: x: 2, y: 2, z: 4, core: 2. Of those that a mesh axis runs over, the one named last changes fastest.
Arguments:
- hidden_in: bfloat16 [16, 4, 64, 5632], P(('groups', 'fsdp'), 'band'), parts along dimension 0, may hold values from -6 to 6
- tap_weights: bfloat16 [9, 5632], P(None, 'fsdp'), may hold values from -2 to 2
- tap_bias: bfloat16 [5632], P('fsdp'), may hold values from -3 to 3
- w_out: bfloat16 [2816, 2240], P('fsdp'), may hold values from -0.109375 to 0.109375
- cotangent: bfloat16 [16, 4, 64, 2240], P(('groups', 'fsdp'), 'band'), parts along dimension 0, may hold values from -0.59765625 to 0.59765625
Outputs:
- block_out: bfloat16 [16, 4, 64, 2240], P(('groups', 'fsdp'), 'band'), parts along dimension 0
- d_hidden: bfloat16 [16, 4, 64, 5632], P(('groups', 'fsdp'), 'band'), parts along dimension 0
- d_taps: float32 [18, 5632], P('groups', 'fsdp'), parts along dimension 0
- d_tap_bias: float32 [11264], P(('groups', 'fsdp')), parts along dimension 0
There are 2 independent parts, one for each index of `groups`. A program takes and returns all parts, laid end to end along the dimension named above; an argument that names none is the same for every part. Nothing has to cross between parts.
All inputs are finite; a program needn't handle non-finite values.
Results may differ from a plain program's by a relative error of at most 0.0049.
Values may be sent and summed in bfloat16 or wider, within the bound.
No kernel may reach another device: no remote copies, remote signals or barrier semaphores. Data moves between devices by JAX's collectives and lax.ppermute only.
A program may use at most 128 MiB of HBM per device.

v0:
```python
import jax
import jax.numpy as jnp
from jax import lax
from jax.sharding import PartitionSpec as P


def with_halo(cells, sides, width):
    for axis, dim in sides:
        count = lax.axis_size(axis)
        ends = count - 1
        head = lax.slice_in_dim(cells, 0, width, axis=dim)
        tail = lax.slice_in_dim(cells, cells.shape[dim] - width, cells.shape[dim], axis=dim)
        cells = jnp.concatenate(
            [
                lax.ppermute(tail, axis, [(i, (i + 1) % count) for i in range(ends)]),
                cells,
                lax.ppermute(head, axis, [((i + 1) % count, i) for i in range(ends)]),
            ],
            axis=dim,
        )
    return cells


def body(hidden_in, tap_weights, tap_bias, w_out, cotangent):
    kernel_all, offset_all = (
        lax.all_gather(tap_weights, "fsdp", axis=1, tiled=True),
        lax.all_gather(tap_bias, "fsdp", axis=0, tiled=True),
    )
    kernel = kernel_all.astype(jnp.float32)
    offset = offset_all.astype(jnp.float32)
    image_count, row_count, col_count, channels = hidden_in.shape
    hidden_units = channels // 2
    token_count = image_count * row_count * col_count
    extended = with_halo(hidden_in, (("band", 1),), 1)
    padded = jnp.pad(extended, ((0, 0), (0, 0), (1, 1), (0, 0)))
    summed = jnp.zeros((image_count, row_count, col_count, channels), jnp.float32) + offset
    for tap_row in range(3):
        for tap_col in range(3):
            window = padded[:, tap_row : tap_row + row_count, tap_col : tap_col + col_count, :]
            summed = summed + kernel[3 * tap_row + tap_col] * window
    values_half = summed[..., :hidden_units]
    gate_half = summed[..., hidden_units:]
    sigmoid_gate = jax.nn.sigmoid(gate_half)
    silu_gate = gate_half * sigmoid_gate
    glu_flat = (values_half * silu_gate).astype(jnp.bfloat16).reshape(token_count, hidden_units)
    grad_flat = cotangent.reshape(token_count, cotangent.shape[3])
    features = grad_flat.shape[1]
    piece = lax.all_gather(w_out, "fsdp", axis=0, tiled=True)
    out_sum = jnp.dot(glu_flat, piece, preferred_element_type=jnp.float32)
    d_piece = lax.dot_general(
        grad_flat, piece, (((1,), (1,)), ((), ())), preferred_element_type=jnp.float32
    )
    out_sum, d_glu = (out_sum, d_piece)
    block_out = out_sum.astype(jnp.bfloat16).reshape(image_count, row_count, col_count, features)
    d_glu = d_glu.reshape(image_count, row_count, col_count, hidden_units)
    slope = sigmoid_gate * (1.0 + gate_half * (1.0 - sigmoid_gate))
    d_pre = jnp.concatenate([d_glu * silu_gate, d_glu * values_half * slope], axis=-1).astype(
        jnp.bfloat16
    )
    d_extended = with_halo(d_pre, (("band", 1),), 1)
    d_pad = jnp.pad(d_extended, ((0, 0), (0, 0), (1, 1), (0, 0)))
    d_image = jnp.zeros((image_count, row_count, col_count, channels), jnp.float32)
    tap_terms = []
    for tap_row in range(3):
        for tap_col in range(3):
            d_window = d_pad[
                :, 2 - tap_row : 2 - tap_row + row_count, 2 - tap_col : 2 - tap_col + col_count, :
            ]
            d_image = d_image + kernel[3 * tap_row + tap_col] * d_window
            window = padded[:, tap_row : tap_row + row_count, tap_col : tap_col + col_count, :]
            tap_terms.append(
                jnp.einsum("srck,srck->k", window, d_pre, preferred_element_type=jnp.float32)
            )
    d_hidden = d_image.astype(jnp.bfloat16)
    tap_grad = jnp.stack(tap_terms)
    bias_grad = jnp.sum(d_pre.astype(jnp.float32), axis=(0, 1, 2))
    tap_grad, bias_grad = lax.psum((tap_grad, bias_grad), "band")
    tap_share, bias_share = (
        lax.psum_scatter(tap_grad, "fsdp", scatter_dimension=1, tiled=True),
        lax.psum_scatter(bias_grad, "fsdp", scatter_dimension=0, tiled=True),
    )
    return (block_out, d_hidden, tap_share, bias_share)


def solution(mesh):
    placed = (
        P(("groups", "fsdp"), "band", None, None),
        P(None, "fsdp"),
        P("fsdp"),
        P("fsdp", None),
        P(("groups", "fsdp"), "band", None, None),
    )
    return jax.shard_map(
        body,
        mesh=mesh,
        in_specs=placed,
        out_specs=(
            P(("groups", "fsdp"), "band", None, None),
            P(("groups", "fsdp"), "band", None, None),
            P("groups", "fsdp"),
            P(("groups", "fsdp")),
        ),
        check_vma=False,
    )
```

profile of v0, /device:TPU:0, one launch (start us, length us, event | category | flops | bytes accessed | tf_op | source)
XLA Modules:
  0.0 235.5 jit_solution(369298379283991862)
XLA Ops:
  7.2 0.0 copy-start
  7.2 0.0 copy-start.22
  7.2 0.0 all-gather.3.cloned.1.call-start
  7.3 0.7 all-gather.3.cloned.1.call-update
  8.0 0.0 reduce-scatter.4.cloned.1.call-start
  8.0 2.6 %fusion.26 = (bf16[1,1,64,5632]{3,2,1,0:T(8,128)(2,1)}, bf16[1,1,64,5632]{3,2,1,0:T(8,128)(2,1)}) fusion(bf16[1,2,64,5632]{3,2,1,0:T(8,128)(2,1)} %param.5), kind=kLoop, calls=%fused_computation.70 | loop fusion | bytes 2883584 | tf_op jit(solution)/shard_map/slice | solution.py:11
  10.6 1.3 collective-permute-start.1
  11.9 5.0 %collective-permute-start = (bf16[1,1,64,5632]{3,2,1,0:T(8,128)(2,1)}, bf16[1,1,64,5632]{3,2,1,0:T(8,128)(2,1)S(1)}, u32[]{:S(2)}, u32[]{:S(2)}) collective-permute-start(bf16[1,1,64,5632]{3,2,1,0:T(8,128)(2,1)} %get-tuple-element.40), channel_id=1, source_target_pairs={{0,1},{2,3},{4,5},{6,7},{8,9},{10,11},{12,13},{14,15},{16,17},{18,... | collective-permute-start | bytes 2162696 | tf_op jit(solution)/shard_map/ppermute | solution.py:15
  16.9 0.6 fusion.27
  18.1 0.2 dynamic-update-slice
  18.4 31.5 %all-reduce.2 = bf16[5632]{0:T(1024)(128)(2,1)S(1)} all-reduce(bf16[5632]{0:T(1024)(128)(2,1)S(1)} %dynamic-update-slice), channel_id=1, replica_groups=mesh['groups'=2,'fsdp'=8,'band'=2] {'fsdp'}, use_global_device_ids=true, to_apply=%add.2 | all-reduce | flops 5632 | bytes 22528
  49.8 0.6 convert_element_type.109
  50.5 25.0 %all-gather = bf16[8,704,9]{1,2,0:T(8,128)(2,1)S(1)} all-gather(bf16[1,704,9]{1,2,0:T(8,128)(2,1)S(1)} %bitcast.101), channel_id=1, replica_groups=mesh['groups'=2,'fsdp'=8,'band'=2] {'fsdp'}, dimensions={0}, use_global_device_ids=true | all-gather | bytes 114048 | tf_op jit(solution)/shard_map/all_gather | solution.py:26
  75.5 0.7 copy_convert_fusion
  76.2 1.8 reshape.190
  78.7 2.4 %slice_reduce_fusion.8 = (f32[5632]{0:T(1024)S(1)}, f32[5632]{0:T(1024)S(1)}, f32[5632]{0:T(1024)S(1)}, f32[5632]{0:T(1024)S(1)}, f32[5632]{0:T(1024)S(1)}, /*in...) fusion(f32[9,5632]{1,0:T(8,128)} %bitcast.97), kind=kLoop, calls=%fused_computation.69 | loop fusion | bytes 405504 | tf_op jit(solution)/shard_map/slice | solution.py:40
  81.2 1.1 select_maximum_fusion.3
  82.3 1.6 copy-done.1
  83.9 3.9 %multiply_add_fusion = f32[1,2,64,5632]{3,2,1,0:T(8,128)} fusion(bf16[1,2,64,5632]{3,2,1,0:T(8,128)(2,1)S(1)} %copy-done.3, f32[5632]{0:T(1024)S(1)} %get-tuple-element.18, f32[5632]{0:T(1024)S(1)} %get-tuple-element.19, f32[5632]{0:T(1024)S(1)} %get-tuple-element.20, f32[5632]{0:T(1024)S(1)} %get-tuple-element.21, f32[5632]{0:T(1024)S(1)} %get-tuple-element.22, ...), kind=kLoop, calls=%fused_computation.39 | loop fusion | flops 20905984 | bytes 14643200 | tf_op jit(solution)/shard_map/add | solution.py:40
  87.8 46.5 %all-gather.3.cloned.1.call-done = bf16[2816,2240]{1,0:T(8,128)(2,1)} async-done(((bf16[352,2240]{1,0:T(8,128)(2,1)}), bf16[2816,2240]{1,0:T(8,128)(2,1)}) %all-gather.3.cloned.1.call-update) | async-done | bytes 12615696 | tf_op jit(solution)/shard_map/all_gather | solution.py:48
  134.3 10.8 %multiply_convert_fusion = (bf16[1,2,64,2816]{3,2,1,0:T(8,128)(2,1)S(1)}, bf16[1,2,64,2816]{3,2,1,0:T(8,128)(2,1)S(1)}, bf16[1,2,64,2816]{3,2,1,0:T(8,128)(2,1)}) fusion(f32[1,2,64,5632]{3,2,1,0:T(8,128)} %multiply_add_fusion, bf16[2816,2240]{1,0:T(8,128)(2,1)} %all-gather.3.cloned.1.call-done, bf16[1,2,64,2240]{3,2,1,0:T(8,128)(2,1)S(1)} %copy-done), kind=kOutput, calls=%fused_computation.52 | convolution fusion | flops 1620213760 | bytes 18235392 | tf_op jit(solution)/shard_map/dot_general | solution.py:50
  145.1 1.2 fusion.23
  146.3 0.2 copy-done.5
  146.5 0.5 copy-done.7
  147.0 3.8 %fusion.19 = (f32[5632]{0:T(1024)S(1)}, f32[5632]{0:T(1024)S(1)}, f32[5632]{0:T(1024)S(1)}, f32[5632]{0:T(1024)S(1)}, f32[5632]{0:T(1024)S(1)}, /*index=5*/f32[5...) fusion(bf16[1,1,64,5632]{3,2,1,0:T(8,128)(2,1)S(1)} %copy-done.5, ...), kind=kLoop, calls=%fused_computation.36 | loop fusion | flops 28785152 | bytes 13178880 | tf_op jit(solution)/shard_map/srck,srck->k/dot_general | solution.py:72
  150.8 0.6 stack.37
  151.4 0.6 stack.31
  152.0 0.6 stack.34
  152.7 0.6 stack.30
  153.3 0.6 stack.32
  153.9 0.6 stack.33
  154.5 0.6 stack.35
  155.2 0.6 stack.36
  155.8 0.6 stack.38
  156.4 3.3 %collective-permute-start.2 = (bf16[1,1,64,5632]{3,2,1,0:T(8,128)(2,1)}, bf16[1,1,64,5632]{3,2,1,0:T(8,128)(2,1)S(1)}, u32[]{:S(2)}, u32[]{:S(2)}) collective-permute-start(bf16[1,1,64,5632]{3,2,1,0:T(8,128)(2,1)} %get-tuple-element.37), channel_id=1, source_target_pairs={{0,1},{2,3},{4,5},{6,7},{8,9},{10,11},{12,13},{14,15},{16,17},{18,... | collective-permute-start | bytes 2162696 | tf_op jit(solution)/shard_map/ppermute | solution.py:15
  159.7 1.5 collective-permute-start.3
  161.2 3.2 %stack.39 = f32[9,5632]{1,0:T(8,128)} concatenate(f32[1,5632]{1,0:T(1,128)} %stack.30, f32[1,5632]{1,0:T(1,128)} %stack.31, f32[1,5632]{1,0:T(1,128)} %stack.32, f32[1,5632]{1,0:T(1,128)} %stack.33, f32[1,5632]{1,0:T(1,128)} %stack.34, f32[1,5632]{1,0:T(1,128)} %stack.35, f32[1,5632]{1,0:T(1,128)} %stack.36, f32[1,5632]{1,0:T(1,128)} %stack.37, f32[1,5632]{1,0:T(1,128)} %stack.38), dimensions={0} | concatenate | bytes 405504 | tf_op jit(solution)/shard_map/stack | solution.py:75
  164.4 3.0 %copy.79 = f32[9,5632]{0,1:T(8,128)} copy(f32[9,5632]{1,0:T(8,128)} %stack.39) | data formatting | bytes 405504
  167.3 0.0 reduce-scatter.4.cloned.1.call-update
  167.3 10.8 %convolution_convert_fusion = bf16[128,2240]{0,1:T(8,128)(2,1)} fusion(bf16[128,2816]{1,0:T(8,128)(2,1)} %bitcast.98, bf16[2816,2240]{1,0:T(8,128)(2,1)} %all-gather.3.cloned.1.call-done), kind=kOutput, calls=%fused_computation.15 | convolution fusion | flops 1615093760 | bytes 13910016 | tf_op jit(solution)/shard_map/dot_general | solution.py:49
  178.2 2.1 copy.15
  180.3 0.8 convert_reduce_fusion
  181.1 27.7 %all-reduce.3 = f32[5632]{0:T(1024)} all-reduce(f32[5632]{0:T(1024)} %convert_reduce_fusion), channel_id=3, replica_groups=mesh['groups'=2,'fsdp'=8,'band'=2] {'fsdp'}, use_global_device_ids=true, to_apply=%region_4.5.clone | all-reduce | flops 5632 | bytes 45056
  208.8 0.8 dynamic-slice.2
  209.6 1.8 copy.80
  211.4 11.0 %all-reduce.4 = (f32[9,704]{1,0:T(8,128)}, f32[704]{0:T(1024)}) all-reduce(f32[9,704]{1,0:T(8,128)} %copy.80, f32[704]{0:T(1024)S(1)} %dynamic-slice.2), channel_id=1, replica_groups=mesh['groups'=2,'fsdp'=8,'band'=2] {'band'}, use_global_device_ids=true, to_apply=%region_0.1 | all-reduce | flops 7040 | bytes 56320 | tf_op jit(solution)/shard_map/psum | solution.py:77
  222.4 1.8 select_maximum_fusion
  224.2 4.5 %fusion.12 = bf16[1,2,64,5632]{3,2,1,0:T(8,128)(2,1)} fusion(bf16[1,4,66,5632]{3,2,1,0:T(8,128)(2,1)S(1)} %select_maximum_fusion, bf16[1,1,64,5632]{3,2,1,0:T(8,128)(2,1)S(1)} %collective-permute-done.2, bf16[1,2,64,2816]{3,2,1,0:T(8,128)(2,1)S(1)} %get-tuple-element.28, bf16[1,2,64,2816]{3,2,1,0:T(8,128)(2,1)S(1)} %get-tuple-element.29, ...), kind=kLoop, calls=%fused_computation.29 | loop fusion | flops 28835840 | bytes 13178880 | tf_op jit(solution)/shard_map/convert_element_type | solution.py:74
  (49 shorter events, 0.1 us)
Async XLA Ops:
  7.2 127.2 %copy-start = (bf16[1,2,64,2240]{3,2,1,0:T(8,128)(2,1)S(1)}, bf16[1,2,64,2240]{3,2,1,0:T(8,128)(2,1)}, u32[]{:S(2)}) copy-start(bf16[1,2,64,2240]{3,2,1,0:T(8,128)(2,1)} %param.9) | copy-start | bytes 1720324
  7.2 9.7 %copy-start.22 = (u32[32]{0:T(128)S(1)}, u32[32]{0:T(128)}, u32[]{:S(2)}) copy-start(u32[32]{0:T(128)} %constant.15) | copy-start | bytes 388
  7.2 73.9 %copy-start.3 = (bf16[1,2,64,5632]{3,2,1,0:T(8,128)(2,1)S(1)}, bf16[1,2,64,5632]{3,2,1,0:T(8,128)(2,1)}, u32[]{:S(2)}) copy-start(bf16[1,2,64,5632]{3,2,1,0:T(8,128)(2,1)} %param.5) | copy-start | bytes 4325380
  7.2 10.9 %copy-start.23 = (bf16[704]{0:T(1024)(128)(2,1)S(1)}, bf16[704]{0:T(1024)(128)(2,1)}, u32[]{:S(2)}) copy-start(bf16[704]{0:T(1024)(128)(2,1)} %param.7) | copy-start | bytes 4228
  7.2 43.2 %copy-start.21 = (bf16[9,704]{1,0:T(8,128)(2,1)S(1)}, bf16[9,704]{1,0:T(8,128)(2,1)}, u32[]{:S(2)}) copy-start(bf16[9,704]{1,0:T(8,128)(2,1)} %param.6) | copy-start | bytes 38020
  7.2 127.1 %all-gather.3.cloned.1.call-start = ((), (), s32[]{:S(2)}) async-start(), calls=%async_computation.1 | async-start | bytes 14598144 | tf_op jit(solution)/shard_map/all_gather | solution.py:48
  8.0 201.7 %reduce-scatter.4.cloned.1.call-start = ((), (), s32[]{:S(2)}) async-start(), calls=%async_computation.2 | async-start | bytes 3244032
  10.6 70.5 %collective-permute-start.1 = (bf16[1,1,64,5632]{3,2,1,0:T(8,128)(2,1)}, bf16[1,1,64,5632]{3,2,1,0:T(8,128)(2,1)S(1)}, u32[]{:S(2)}, u32[]{:S(2)}) collective-permute-start(bf16[1,1,64,5632]{3,2,1,0:T(8,128)(2,1)} %get-tuple-element.39), channel_id=1, source_target_pairs={{1,0},{3,2},{5,4},{7,6},{9,8},{11,10},{13,12},{15,14},{17,16},{19,... | collective-permute-start | bytes 2162696 | tf_op jit(solution)/shard_map/ppermute | solution.py:17
  11.9 69.3 %collective-permute-start = (bf16[1,1,64,5632]{3,2,1,0:T(8,128)(2,1)}, bf16[1,1,64,5632]{3,2,1,0:T(8,128)(2,1)S(1)}, u32[]{:S(2)}, u32[]{:S(2)}) collective-permute-start(bf16[1,1,64,5632]{3,2,1,0:T(8,128)(2,1)} %get-tuple-element.40), channel_id=1, source_target_pairs={{0,1},{2,3},{4,5},{6,7},{8,9},{10,11},{12,13},{14,15},{16,17},{18,... | collective-permute-start | bytes 2162696 | tf_op jit(solution)/shard_map/ppermute | solution.py:15
  81.0 1.2 copy-start.8
  81.0 1.2 copy-start.10
  81.1 1.2 copy-start.12
  81.1 1.2 copy-start.14
  81.1 1.2 copy-start.16
  81.1 1.2 copy-start.18
  81.1 2.8 %copy-start.20 = (f32[5632]{0:T(1024)S(1)}, f32[5632]{0:T(1024)}, u32[]{:S(2)}) copy-start(f32[5632]{0:T(1024)} %convert_element_type.109) | copy-start | bytes 67588
  81.1 1.2 copy-start.4
  81.2 1.2 copy-start.6
  82.2 1.7 copy-start.1
  134.3 12.0 %copy-start.2 = (bf16[1,4,66,5632]{3,2,1,0:T(8,128)(2,1)S(1)}, bf16[1,4,66,5632]{3,2,1,0:T(8,128)(2,1)}, u32[]{:S(2)}) copy-start(bf16[1,4,66,5632]{3,2,1,0:T(8,128)(2,1)} %copy-done.1) | copy-start | bytes 8921092
  145.1 1.4 copy-start.5
  145.1 1.8 copy-start.7
  156.4 66.0 %collective-permute-start.2 = (bf16[1,1,64,5632]{3,2,1,0:T(8,128)(2,1)}, bf16[1,1,64,5632]{3,2,1,0:T(8,128)(2,1)S(1)}, u32[]{:S(2)}, u32[]{:S(2)}) collective-permute-start(bf16[1,1,64,5632]{3,2,1,0:T(8,128)(2,1)} %get-tuple-element.37), channel_id=1, source_target_pairs={{0,1},{2,3},{4,5},{6,7},{8,9},{10,11},{12,13},{14,15},{16,17},{18,... | collective-permute-start | bytes 2162696 | tf_op jit(solution)/shard_map/ppermute | solution.py:15
  159.7 62.7 %collective-permute-start.3 = (bf16[1,1,64,5632]{3,2,1,0:T(8,128)(2,1)}, bf16[1,1,64,5632]{3,2,1,0:T(8,128)(2,1)S(1)}, u32[]{:S(2)}, u32[]{:S(2)}) collective-permute-start(bf16[1,1,64,5632]{3,2,1,0:T(8,128)(2,1)} %get-tuple-element.38), channel_id=1, source_target_pairs={{1,0},{3,2},{5,4},{7,6},{9,8},{11,10},{13,12},{15,14},{17,16},{19,... | collective-permute-start | bytes 2162696 | tf_op jit(solution)/shard_map/ppermute | solution.py:17
  222.3 1.8 copy-start.9
  222.3 1.8 copy-start.11
  222.3 1.8 copy-start.13
  222.3 1.8 copy-start.15
  222.3 1.8 copy-start.17
  222.4 1.8 copy-start.19
Sparse Core Ops, SparseCore 0:
  9.7 124.6 all-gather.2
  167.5 38.8 reduce-scatter.3
where the time goes:
time: 236 us
  blocking collectives  95.2 us (40%)
  waiting for transfers between devices  47.2 us (20%)
  local copies, waits for them, and re-layouts  26.3 us (11%)
  matrix products  21.6 us (9%)
  other arithmetic  18.4 us (8%)
  between operations  15.7 us (7%)
  starting transfers between devices  11.1 us (5%)
    unnamed x2, blocking collectives  59.2 us
    all_gather x1, waiting for transfers between devices, body(): piece = lax.all_gather(w_out, 'fsdp', axis=0, tiled=True)  46.5 us
    all_gather x1, blocking collectives, body(): lax.all_gather(tap_weights, 'fsdp', axis=1, tiled=True)  25 us
    psum x1, blocking collectives, body(): tap_grad, bias_grad = lax.psum((tap_grad, bias_grad), 'band')  11 us
    dot_general x1, matrix products, body(): out_sum = jnp.dot(glu_flat, piece, preferred_element_type=jnp.float32)  10.8 us
    dot_general x1, matrix products, body(): lax.dot_general(grad_flat, piece, (((1,), (1,)), ((), ())), preferred_ele...  10.8 us
    another operation x10, local copies, waits for them, and re-layouts, body(): tap_grad = jnp.stack(tap_terms)  8.77 us
    unnamed x54, local copies, waits for them, and re-layouts  8.64 us
  transfers between devices with their start and end apart: 6, of which 1 were waited for; matrix products, arithmetic and copies ran while one was open for 15% of the time, Pallas kernels for 0%

commit v1 on v0

--- a/solution.py
+++ b/solution.py
@@ -2,6 +2,18 @@
 import jax.numpy as jnp
 from jax import lax
 from jax.sharding import PartitionSpec as P
+
+
+def gather_by_bits(x, axis, dim):
+    ways, here = (lax.axis_size(axis), lax.axis_index(axis))
+    grown, reach = (x, 1)
+    while reach < ways:
+        theirs = lax.ppermute(grown, axis, [(d, d ^ reach) for d in range(ways)])
+        mine_first = jnp.concatenate([grown, theirs], axis=dim)
+        theirs_first = jnp.concatenate([theirs, grown], axis=dim)
+        grown = jnp.where(here & reach == 0, mine_first, theirs_first)
+        reach = 2 * reach
+    return grown
 
 
 def with_halo(cells, sides, width):
@@ -45,7 +57,7 @@
     glu_flat = (values_half * silu_gate).astype(jnp.bfloat16).reshape(token_count, hidden_units)
     grad_flat = cotangent.reshape(token_count, cotangent.shape[3])
     features = grad_flat.shape[1]
-    piece = lax.all_gather(w_out, "fsdp", axis=0, tiled=True)
+    piece = gather_by_bits(w_out, "fsdp", 0)
     out_sum = jnp.dot(glu_flat, piece, preferred_element_type=jnp.float32)
     d_piece = lax.dot_general(
         grad_flat, piece, (((1,), (1,)), ((), ())), preferred_element_type=jnp.float32

time: 236 us -> 534 us (2.26)
  blocking collectives: 95.2 us -> 334 us
  waiting for transfers between devices: 47.2 us -> 74.2 us
  other arithmetic: 18.4 us -> 35 us
  starting transfers between devices: 11.1 us -> 18.7 us
    all_gather x1, blocking collectives: 25 us -> 274 us  [body(): lax.all_gather(tap_weights, 'fsdp', axis=1, tiled=True)]
    ppermute x0 -> x3, waiting for transfers between devices: none -> 74.1 us  [gather_by_bits(): theirs = lax.ppermute(grown, axis, [(d, d ^ reach) for d in range(ways)])]
    all_gather x1 -> x0, waiting for transfers between devices: 46.5 us -> none  [body(): piece = lax.all_gather(w_out, 'fsdp', axis=0, tiled=True)]
    select_n x0 -> x2, other arithmetic: none -> 13.2 us  [gather_by_bits(): grown = jnp.where(here & reach == 0, mine_first, theirs_first)]
    select_n x0 -> x1, local copies, waits for them, and re-layouts: none -> 9.47 us  [gather_by_bits(): grown = jnp.where(here & reach == 0, mine_first, theirs_first)]
    ppermute x0 -> x1, local copies, waits for them, and re-layouts: none -> 9.31 us  [gather_by_bits(): theirs = lax.ppermute(grown, axis, [(d, d ^ reach) for d in range(ways)])]
    another operation x10, local copies, waits for them, and re-layouts: 8.77 us -> 0.46 us  [body(): tap_grad = jnp.stack(tap_terms)]
    unnamed x2, blocking collectives: 59.2 us -> 52.4 us
  transfers between devices with their start and end apart: 6 -> 8, of which waited for: 1 -> 2; matrix products, arithmetic and copies ran while one was open for 15% -> 7% of each run, Pallas kernels for 0% -> 0%
where the time goes in v1:
time: 534 us
  blocking collectives  334 us (63%)
  waiting for transfers between devices  74.2 us (14%)
  other arithmetic  35 us (7%)
  local copies, waits for them, and re-layouts  31.3 us (6%)
  matrix products  24.7 us (5%)
  starting transfers between devices  18.7 us (4%)
  between operations  15.8 us (3%)
    all_gather x1, blocking collectives, body(): lax.all_gather(tap_weights, 'fsdp', axis=1, tiled=True)  274 us
    ppermute x3, waiting for transfers between devices, gather_by_bits(): theirs = lax.ppermute(grown, axis, [(d, d ^ reach) for d in range(ways)])  74.1 us
    unnamed x2, blocking collectives  52.4 us
    select_n x2, other arithmetic, gather_by_bits(): grown = jnp.where(here & reach == 0, mine_first, theirs_first)  13.2 us
    dot_general x1, matrix products, body(): out_sum = jnp.dot(glu_flat, piece, preferred_element_type=jnp.float32)  13 us
    dot_general x1, matrix products, body(): lax.dot_general(grad_flat, piece, (((1,), (1,)), ((), ())), preferred_ele...  11.7 us
  transfers between devices with their start and end apart: 8, of which 2 were waited for; matrix products, arithmetic and copies ran while one was open for 7% of the time, Pallas kernels for 0%

profile of v1, /device:TPU:0, one launch (start us, length us, event | category | flops | bytes accessed | tf_op | source)
XLA Modules:
  0.0 533.6 jit_solution(10792565081676744686)
XLA Ops:
  7.2 0.0 copy-start
  7.2 0.0 reduce-scatter.4.cloned.1.call-start
  7.2 0.6 collective-permute-start.2
  7.8 3.3 collective-permute-done.2
  11.1 4.0 maximum_select_fusion.2
  15.1 2.9 collective-permute-start.3
  18.0 70.8 %collective-permute-done.3 = bf16[704,2240]{1,0:T(8,128)(2,1)} collective-permute-done((bf16[704,2240]{1,0:T(8,128)(2,1)}, bf16[704,2240]{1,0:T(8,128)(2,1)}, u32[]{:S(2)}, u32[]{:S(2)}) %collective-permute-start.3) | collective-permute-done | bytes 3153952 | tf_op jit(solution)/shard_map/ppermute | solution.py:11
  88.8 9.2 %maximum_select_fusion.1 = bf16[1408,2240]{1,0:T(8,128)(2,1)} fusion(bf16[704,2240]{1,0:T(8,128)(2,1)} %collective-permute-done.3, bf16[704,2240]{1,0:T(8,128)(2,1)} %maximum_select_fusion.2, pred[]{:T(512)S(6)} %eq.10), kind=kLoop, calls=%fused_computation.12 | loop fusion | flops 28385280 | bytes 12615681 | tf_op jit(solution)/shard_map/jit(_where)/select_n | solution.py:14
  98.0 9.5 %copy.23 = bf16[1408,2240]{0,1:T(8,128)(2,1)} copy(bf16[1408,2240]{1,0:T(8,128)(2,1)} %maximum_select_fusion.1) | data formatting | bytes 12615680 | tf_op jit(solution)/shard_map/jit(_where)/select_n | solution.py:14
  107.5 2.8 collective-permute-start.4
  110.3 1.2 fusion.23
  111.5 3.4 collective-permute-start
  115.0 1.3 collective-permute-start.1
  116.3 273.7 %all-gather = bf16[8,704,9]{1,2,0:T(8,128)(2,1)S(1)} all-gather(bf16[1,704,9]{1,2,0:T(8,128)(2,1)S(1)} %bitcast.93), channel_id=1, replica_groups=mesh['groups'=2,'fsdp'=8,'band'=2] {'fsdp'}, dimensions={0}, use_global_device_ids=true | all-gather | bytes 114048 | tf_op jit(solution)/shard_map/all_gather | solution.py:38
  390.0 0.7 copy_convert_fusion
  390.7 1.8 reshape.189
  392.5 0.6 fusion.24
  393.8 0.2 dynamic-update-slice
  394.0 26.2 %all-reduce.2 = bf16[5632]{0:T(1024)(128)(2,1)S(1)} all-reduce(bf16[5632]{0:T(1024)(128)(2,1)S(1)} %dynamic-update-slice), channel_id=1, replica_groups=mesh['groups'=2,'fsdp'=8,'band'=2] {'fsdp'}, use_global_device_ids=true, to_apply=%add.2 | all-reduce | flops 5632 | bytes 22528
  420.2 0.6 convert_element_type.109
  421.5 2.7 slice_reduce_fusion.8
  424.3 0.0 copy-start.22
  424.3 0.0 collective-permute-done
  424.3 0.0 collective-permute-done.1
  424.3 1.1 select_maximum_fusion.3
  425.5 4.0 multiply_add_fusion
  429.5 9.3 %copy.24 = bf16[1408,2240]{1,0:T(8,128)(2,1)} copy(bf16[1408,2240]{0,1:T(8,128)(2,1)} %collective-permute-done.4) | data formatting | bytes 12615680 | tf_op jit(solution)/shard_map/ppermute | solution.py:11
  438.8 11.7 %fusion.17 = f32[2816,128]{0,1:T(8,128)S(1)} fusion(bf16[128,2240]{1,0:T(8,128)(2,1)S(1)} %bitcast.84, bf16[1408,2240]{1,0:T(8,128)(2,1)} %copy.24, bf16[1408,2240]{1,0:T(8,128)(2,1)} %maximum_select_fusion.1, pred[]{:T(512)S(6)} %eq.9), kind=kOutput, calls=%fused_computation.40 | convolution fusion | flops 1671577600 | bytes 14630913 | tf_op jit(solution)/shard_map/dot_general | solution.py:62
  450.5 1.7 multiply_convert_fusion
  452.1 1.2 fusion.19
  453.3 1.3 collective-permute-start.6
  454.6 6.3 %collective-permute-start.5 = (bf16[1,1,64,5632]{3,2,1,0:T(8,128)(2,1)}, bf16[1,1,64,5632]{3,2,1,0:T(8,128)(2,1)}, u32[]{:S(2)}, u32[]{:S(2)}) collective-permute-start(bf16[1,1,64,5632]{3,2,1,0:T(8,128)(2,1)} %get-tuple-element.37), channel_id=1, source_target_pairs={{0,1},{2,3},{4,5},{6,7},{8,9},{10,11},{12,13},{14,15},{16,17},{18,... | collective-permute-start | bytes 2162696 | tf_op jit(solution)/shard_map/ppermute | solution.py:27
  460.9 3.8 fusion.14
  465.0 0.3 stack.39
  465.3 0.0 copy-start.9
  465.3 2.1 copy.90
  467.4 0.0 reduce-scatter.4.cloned.1.call-update
  467.5 13.0 %convolution_convert_fusion = bf16[128,2240]{0,1:T(8,128)(2,1)} fusion(bf16[128,2816]{1,0:T(8,128)(2,1)S(1)} %bitcast.90, bf16[1408,2240]{1,0:T(8,128)(2,1)} %copy.24, bf16[1408,2240]{1,0:T(8,128)(2,1)} %maximum_select_fusion.1, pred[]{:T(512)S(6)} %eq.9), kind=kOutput, calls=%fused_computation.14 | convolution fusion | flops 1671864320 | bytes 13910017 | tf_op jit(solution)/shard_map/dot_general | solution.py:61
  480.5 2.1 copy.26
  482.6 0.2 convert_reduce_fusion
  482.8 26.2 %all-reduce.3 = f32[5632]{0:T(1024)S(1)} all-reduce(f32[5632]{0:T(1024)S(1)} %convert_reduce_fusion), channel_id=3, replica_groups=mesh['groups'=2,'fsdp'=8,'band'=2] {'fsdp'}, use_global_device_ids=true, to_apply=%region_4.5.clone | all-reduce | flops 5632 | bytes 45056
  509.0 0.1 dynamic-slice.2
  509.1 1.1 copy.91
  510.2 7.8 %all-reduce.4 = (f32[9,704]{1,0:T(8,128)}, f32[704]{0:T(1024)}) all-reduce(f32[9,704]{1,0:T(8,128)S(1)} %copy.91, f32[704]{0:T(1024)S(1)} %dynamic-slice.2), channel_id=1, replica_groups=mesh['groups'=2,'fsdp'=8,'band'=2] {'band'}, use_global_device_ids=true, to_apply=%region_0.1 | all-reduce | flops 7040 | bytes 56320 | tf_op jit(solution)/shard_map/psum | solution.py:89
  518.1 0.0 collective-permute-done.6
  518.1 0.0 collective-permute-done.5
  518.1 2.9 select_maximum_fusion
  521.0 5.7 %fusion.7 = bf16[1,2,64,5632]{3,2,1,0:T(8,128)(2,1)} fusion(bf16[1,4,66,5632]{3,2,1,0:T(8,128)(2,1)S(1)} %select_maximum_fusion, bf16[1,1,64,5632]{3,2,1,0:T(8,128)(2,1)} %collective-permute-done.5, bf16[1,2,64,2816]{3,2,1,0:T(8,128)(2,1)S(1)} %get-tuple-element.28, bf16[1,2,64,2816]{3,2,1,0:T(8,128)(2,1)S(1)} %get-tuple-element.29, ...), kind=kLoop, calls=%fused_computation.29 | loop fusion | flops 28835840 | bytes 13178880 | tf_op jit(solution)/shard_map/convert_element_type | solution.py:86
  (61 shorter events, 0.3 us)
Async XLA Ops:
  7.2 431.6 %copy-start = (bf16[1,2,64,2240]{3,2,1,0:T(8,128)(2,1)S(1)}, bf16[1,2,64,2240]{3,2,1,0:T(8,128)(2,1)}, u32[]{:S(2)}) copy-start(bf16[1,2,64,2240]{3,2,1,0:T(8,128)(2,1)} %param.9) | copy-start | bytes 1720324
  7.2 501.9 %reduce-scatter.4.cloned.1.call-start = ((), (), s32[]{:S(2)}) async-start(), calls=%async_computation.1 | async-start | bytes 3244032
  7.2 3.9 collective-permute-start.2
  15.1 73.8 %collective-permute-start.3 = (bf16[704,2240]{1,0:T(8,128)(2,1)}, bf16[704,2240]{1,0:T(8,128)(2,1)}, u32[]{:S(2)}, u32[]{:S(2)}) collective-permute-start(bf16[704,2240]{1,0:T(8,128)(2,1)} %maximum_select_fusion.2), channel_id=1, source_target_pairs={{0,4},{2,6},{4,0},{6,2},{8,12},{10,14},{12,8},{14,10},{1,5},{3,7},... | collective-permute-start | bytes 9461768 | tf_op jit(solution)/shard_map/ppermute | solution.py:11
  98.0 12.3 %copy-start.3 = (bf16[1,2,64,5632]{3,2,1,0:T(8,128)(2,1)S(1)}, bf16[1,2,64,5632]{3,2,1,0:T(8,128)(2,1)}, u32[]{:S(2)}) copy-start(bf16[1,2,64,5632]{3,2,1,0:T(8,128)(2,1)} %param.5) | copy-start | bytes 4325380
  107.5 8.8 %copy-start.23 = (bf16[9,704]{1,0:T(8,128)(2,1)S(1)}, bf16[9,704]{1,0:T(8,128)(2,1)}, u32[]{:S(2)}) copy-start(bf16[9,704]{1,0:T(8,128)(2,1)} %param.6) | copy-start | bytes 38020
  107.5 285.0 %copy-start.24 = (u32[32]{0:T(128)S(1)}, u32[32]{0:T(128)}, u32[]{:S(2)}) copy-start(u32[32]{0:T(128)} %constant.28) | copy-start | bytes 388
  107.5 286.3 %copy-start.25 = (bf16[704]{0:T(1024)(128)(2,1)S(1)}, bf16[704]{0:T(1024)(128)(2,1)}, u32[]{:S(2)}) copy-start(bf16[704]{0:T(1024)(128)(2,1)} %param.7) | copy-start | bytes 4228
  107.5 321.9 %collective-permute-start.4 = (bf16[1408,2240]{0,1:T(8,128)(2,1)}, bf16[1408,2240]{0,1:T(8,128)(2,1)}, u32[]{:S(2)}, u32[]{:S(2)}) collective-permute-start(bf16[1408,2240]{0,1:T(8,128)(2,1)} %copy.23), channel_id=1, source_target_pairs={{0,8},{2,10},{4,12},{6,14},{8,0},{10,2},{12,4},{14,6},{1,9},{3,11}... | collective-permute-start | bytes 18923528 | tf_op jit(solution)/shard_map/ppermute | solution.py:11
  111.5 312.7 %collective-permute-start = (bf16[1,1,64,5632]{3,2,1,0:T(8,128)(2,1)}, bf16[1,1,64,5632]{3,2,1,0:T(8,128)(2,1)S(1)}, u32[]{:S(2)}, u32[]{:S(2)}) collective-permute-start(bf16[1,1,64,5632]{3,2,1,0:T(8,128)(2,1)} %get-tuple-element.40), channel_id=1, source_target_pairs={{0,1},{2,3},{4,5},{6,7},{8,9},{10,11},{12,13},{14,15},{16,17},{18,... | collective-permute-start | bytes 2162696 | tf_op jit(solution)/shard_map/ppermute | solution.py:27
  115.0 309.3 %collective-permute-start.1 = (bf16[1,1,64,5632]{3,2,1,0:T(8,128)(2,1)}, bf16[1,1,64,5632]{3,2,1,0:T(8,128)(2,1)S(1)}, u32[]{:S(2)}, u32[]{:S(2)}) collective-permute-start(bf16[1,1,64,5632]{3,2,1,0:T(8,128)(2,1)} %get-tuple-element.39), channel_id=1, source_target_pairs={{1,0},{3,2},{5,4},{7,6},{9,8},{11,10},{13,12},{15,14},{17,16},{19,... | collective-permute-start | bytes 2162696 | tf_op jit(solution)/shard_map/ppermute | solution.py:29
  424.2 1.2 copy-start.10
  424.2 1.2 copy-start.12
  424.2 1.2 copy-start.14
  424.2 1.2 copy-start.16
  424.2 1.2 copy-start.18
  424.2 1.2 copy-start.20
  424.3 1.2 copy-start.22
  424.3 1.2 copy-start.5
  424.3 1.2 copy-start.7
  425.4 4.1 copy-start.1
  438.8 11.7 %copy-start.4 = (f32[1,2,64,5632]{3,2,1,0:T(8,128)S(1)}, f32[1,2,64,5632]{3,2,1,0:T(8,128)}, u32[]{:S(2)}) copy-start(f32[1,2,64,5632]{3,2,1,0:T(8,128)} %multiply_add_fusion) | copy-start | bytes 8650756
  450.5 10.5 %copy-start.2 = (bf16[1,4,66,5632]{3,2,1,0:T(8,128)(2,1)S(1)}, bf16[1,4,66,5632]{3,2,1,0:T(8,128)(2,1)}, u32[]{:S(2)}) copy-start(bf16[1,4,66,5632]{3,2,1,0:T(8,128)(2,1)} %copy-done.1) | copy-start | bytes 8921092
  452.1 8.8 %copy-start.6 = (bf16[1,1,64,5632]{3,2,1,0:T(8,128)(2,1)S(1)}, bf16[1,1,64,5632]{3,2,1,0:T(8,128)(2,1)}, u32[]{:S(2)}) copy-start(bf16[1,1,64,5632]{3,2,1,0:T(8,128)(2,1)} %copy-done.5) | copy-start | bytes 2162692
  452.1 8.8 %copy-start.8 = (bf16[1,1,64,5632]{3,2,1,0:T(8,128)(2,1)S(1)}, bf16[1,1,64,5632]{3,2,1,0:T(8,128)(2,1)}, u32[]{:S(2)}) copy-start(bf16[1,1,64,5632]{3,2,1,0:T(8,128)(2,1)} %copy-done.7) | copy-start | bytes 2162692
  453.3 64.7 %collective-permute-start.6 = (bf16[1,1,64,5632]{3,2,1,0:T(8,128)(2,1)}, bf16[1,1,64,5632]{3,2,1,0:T(8,128)(2,1)}, u32[]{:S(2)}, u32[]{:S(2)}) collective-permute-start(bf16[1,1,64,5632]{3,2,1,0:T(8,128)(2,1)} %get-tuple-element.38), channel_id=1, source_target_pairs={{1,0},{3,2},{5,4},{7,6},{9,8},{11,10},{13,12},{15,14},{17,16},{19,... | collective-permute-start | bytes 2162696 | tf_op jit(solution)/shard_map/ppermute | solution.py:29
  454.6 63.5 %collective-permute-start.5 = (bf16[1,1,64,5632]{3,2,1,0:T(8,128)(2,1)}, bf16[1,1,64,5632]{3,2,1,0:T(8,128)(2,1)}, u32[]{:S(2)}, u32[]{:S(2)}) collective-permute-start(bf16[1,1,64,5632]{3,2,1,0:T(8,128)(2,1)} %get-tuple-element.37), channel_id=1, source_target_pairs={{0,1},{2,3},{4,5},{6,7},{8,9},{10,11},{12,13},{14,15},{16,17},{18,... | collective-permute-start | bytes 2162696 | tf_op jit(solution)/shard_map/ppermute | solution.py:27
  465.3 2.1 copy-start.9
  518.0 2.9 copy-start.11
  518.0 2.9 copy-start.13
  518.1 2.9 copy-start.15
  518.1 3.0 copy-start.17
  518.1 3.0 copy-start.19
  518.1 3.0 copy-start.21
Sparse Core Ops, SparseCore 0:
  467.6 36.4 reduce-scatter.3
